TPU v7x, 128 devices: a whole 4x4x4 slice. The times are simulated.
128 devices in a mesh: cube: 128 (over x, z, y, core).
Axes of the slice: x: 4, y: 4, z: 4, core: 2. Of those that a mesh axis runs over, the one named last changes fastest.
Arguments:
- gfront: float32 [8192, 2048], P('cube'), as said below
- cfront: float32 [8192, 4096], P('cube'), as said below
- rfront: float32 [8192, 8192], P('cube'), as said below
- gmap: int32 [4, 2048], replicated, may hold values from 0 to 4095, as said below
- cmap: int32 [2, 4096], replicated, may hold values from 0 to 8191, as said below
Outputs:
- gfactor: float32 [8192, 256], P('cube')
- cfactor: float32 [8192, 256], P('cube')
- rfactor: float32 [8192, 512], P('cube')
- rschur: float32 [8192, 8192], P('cube')
Inputs may be any that keep to these rules, and one draw needn't show every extreme that they name: Entry i of row q goes to a row of the parent front in block b or block b + 32, where b = i // 64 and blocks have 64 rows; within one row of gmap the entries are distinct and increase along each block. Entry i of row c goes to a row of the root front in block b or block b + 64, where b = i // 64 and blocks have 64 rows; within one row of cmap the entries are distinct and increase along each block. `gfront`: every front is symmetric and positive definite. `cfront`: every front is symmetric and positive definite. `rfront`: the front is symmetric and positive definite.
All inputs are finite; a program needn't handle non-finite values.
Results may differ from a plain program's by a relative error of at most 0.0003.
Values sent between devices are 32-bit elements; how exact they have to be, the bound alone decides.
A program may use at most 128 MiB of HBM per device.

v0:
```python
import jax
import jax.numpy as jnp
from jax import lax
from jax.sharding import PartitionSpec as P

TILE = 256
PG = 1
PC = 1
PR = 2


def from_partner(value, axis, bit):
    mask = 2**bit
    pairs = [(source, source ^ mask) for source in range(lax.axis_size(axis))]
    return lax.ppermute(value, axis, pairs)


def share_panel(own_cols, group):
    device_idx = lax.axis_index("cube")
    everything = lax.all_gather(own_cols, "cube", axis=0, tiled=True)
    row_count = own_cols.shape[0]
    start_row = device_idx // group * group * row_count
    return lax.dynamic_slice_in_dim(everything, start_row, group * row_count, 0)


def kept_index(index_vals, order, separator):
    return (index_vals < order - separator - TILE) | (index_vals >= order - TILE)


def eliminate(rows_mat, panels, group):
    row_count = rows_mat.shape[0]
    order = rows_mat.shape[1]
    start = order - (panels + 1) * TILE
    device_idx = lax.axis_index("cube")
    row_ids = device_idx % group * row_count + jnp.arange(row_count, dtype=jnp.int32)
    col_ids = jnp.arange(order, dtype=jnp.int32)
    pieces = []
    for panel_no in range(panels):
        col_low = start + panel_no * TILE
        col_high = col_low + TILE
        own_cols = rows_mat[:, col_low:col_high]
        whole_panel = share_panel(own_cols, group)
        lower_tri = jnp.linalg.cholesky(whole_panel[col_low:col_high])
        weights = jax.scipy.linalg.cho_solve((lower_tri, True), own_cols.T).T
        factor = jax.scipy.linalg.solve_triangular(lower_tri, own_cols.T, lower=True).T
        pieces.append(jnp.where(((row_ids >= col_low) | (row_ids < start))[:, None], factor, 0.0))
        product = jnp.einsum("rb,nb->rn", weights, whole_panel, precision=lax.Precision.HIGHEST)
        row_rest = (row_ids >= col_high) | (row_ids < start)
        col_rest = (col_ids >= col_high) | (col_ids < start)
        trailing = row_rest[:, None] & col_rest[None, :]
        rows_mat = rows_mat - jnp.where(trailing, product, 0.0)
    return (rows_mat, jnp.concatenate(pieces, 1))


def extend_add(rows_mat, separator, maps_all, group):
    row_count = rows_mat.shape[0]
    order = rows_mat.shape[1]
    pair_bit = group.bit_length() - 1
    device_idx = lax.axis_index("cube")
    block_no = device_idx % group
    front_no = device_idx // group
    side = front_no % 2
    row_ids = block_no * row_count + jnp.arange(row_count, dtype=jnp.int32)
    col_ids = jnp.arange(order, dtype=jnp.int32)
    keep_mask = (
        kept_index(row_ids, order, separator)[:, None]
        & kept_index(col_ids, order, separator)[None, :]
    )
    masked = jnp.where(keep_mask, rows_mat, 0.0)
    own_map = lax.dynamic_index_in_dim(maps_all, front_no, 0, keepdims=False)
    widened = jnp.zeros((row_count, 2 * order), jnp.float32).at[:, own_map].add(masked)
    row_map = lax.dynamic_slice_in_dim(own_map, block_no * row_count, row_count, 0)
    slots = jnp.where(
        row_map < (block_no + 1) * row_count,
        row_map - block_no * row_count,
        row_map - (group + block_no) * row_count + row_count,
    )
    own_pair = jnp.zeros((2 * row_count, 2 * order), jnp.float32).at[slots].add(widened)
    kept_rows = lax.dynamic_slice_in_dim(own_pair, side * row_count, row_count, 0)
    outgoing = lax.dynamic_slice_in_dim(own_pair, (1 - side) * row_count, row_count, 0)
    received = from_partner(outgoing, "cube", pair_bit)
    return (kept_rows, received)


def local(gfront, cfront, rfront, gmap, cmap):
    devices = lax.axis_size("cube")
    quarter = devices // 4
    half_cube = devices // 2
    g_rows, gfactor = eliminate(gfront, PG, quarter)
    kept_rows, received = extend_add(g_rows, PG * TILE, gmap, quarter)
    c_rows = cfront + kept_rows + received
    c_done, cfactor = eliminate(c_rows, PC, half_cube)
    kept_rows, received = extend_add(c_done, PC * TILE, cmap, half_cube)
    r_rows = rfront + kept_rows + received
    r_done, rfactor = eliminate(r_rows, PR, devices)
    row_count = r_done.shape[0]
    order = r_done.shape[1]
    row_ids = lax.axis_index("cube") * row_count + jnp.arange(row_count, dtype=jnp.int32)
    col_ids = jnp.arange(order, dtype=jnp.int32)
    rest_mask = (
        kept_index(row_ids, order, PR * TILE)[:, None]
        & kept_index(col_ids, order, PR * TILE)[None, :]
    )
    rschur = jnp.where(rest_mask, r_done, 0.0)
    return (gfactor, cfactor, rfactor, rschur)


def solution(mesh):
    placed = (P("cube", None), P("cube", None), P("cube", None), P(), P())
    return jax.shard_map(
        local,
        mesh=mesh,
        in_specs=placed,
        out_specs=(P("cube", None), P("cube", None), P("cube", None), P("cube", None)),
        check_vma=False,
    )
```

profile of v0, /device:TPU:1, one launch (start us, length us, event | category | flops | bytes accessed | tf_op | source)
XLA Modules:
  0.0 717.6 jit_solution(15495992627534233926)
XLA Ops:
  10.4 74.4 %all-gather.5.cloned.1.call-done = f32[8192,256]{1,0:T(8,128)} async-done(((f32[64,256]{1,0:T(8,128)}), f32[8192,256]{1,0:T(8,128)}) %all-gather.5.cloned.1.call-update) | async-done | bytes 8388624 | tf_op jit(solution)/shard_map/all_gather | solution.py:20
  87.0 11.7 %cholesky.214 = f32[128,128]{1,0:T(8,128)S(1)} custom-call(f32[128,128]{1,0:T(8,128)S(1)} %cholesky.346), custom_call_target="Cholesky" | custom-call | tf_op jit(solution)/shard_map/jit(cholesky)/cholesky | solution.py:43
  98.8 9.8 %custom-call.31 = f32[1,128,128]{1,2,0:T(8,128)S(1)} custom-call(f32[1,128,128]{2,1,0:T(8,128)S(1)} %get-tuple-element.170), custom_call_target="InvertDiagBlocksLowerTriangular" | custom-call | tf_op jit(solution)/shard_map/jit(cholesky)/cholesky | solution.py:43
  109.1 11.7 %cholesky.231 = f32[128,128]{1,0:T(8,128)S(1)} custom-call(f32[128,128]{1,0:T(8,128)S(1)} %convolution_subtract_fusion.3), custom_call_target="Cholesky" | custom-call | tf_op jit(solution)/shard_map/jit(cholesky)/cholesky | solution.py:43
  122.9 4.2 while.28
  127.1 19.7 %custom-call.32 = f32[2,128,128]{1,2,0:T(8,128)S(1)} custom-call(f32[2,128,128]{2,1,0:T(8,128)S(1)} %get-tuple-element.87), custom_call_target="InvertDiagBlocksLowerTriangular" | custom-call | tf_op jit(solution)/shard_map/jit(_solve_triangular)/triangular_solve/custom-call.1 | solution.py:45
  152.2 12.0 %scatter_custom_fusion = f32[64,4096]{0,1:T(8,128)S(1)} fusion(s32[2048]{0:T(1024)S(1)} %bitcast.226, f32[2048,64]{1,0:T(8,128)S(1)} %copy.42, f32[]{:T(128)} %constant.212.clone.1), kind=kCustom, calls=%fused_computation.41 | custom fusion | flops 131072 | bytes 1048580 | tf_op jit(solution)/shard_map/scatter-add | solution.py:71
  167.4 24.5 %collective-permute-done = f32[64,4096]{1,0:T(8,128)} collective-permute-done((f32[64,4096]{1,0:T(8,128)S(1)}, f32[64,4096]{1,0:T(8,128)}, u32[]{:S(2)}, u32[]{:S(2)}) %collective-permute-start) | collective-permute-done | bytes 1048608 | tf_op jit(solution)/shard_map/ppermute | solution.py:15
  194.9 67.5 %all-gather.7.cloned.1.call-done = f32[8192,256]{1,0:T(8,128)} async-done(((f32[64,256]{1,0:T(8,128)}), f32[8192,256]{1,0:T(8,128)}) %all-gather.7.cloned.1.call-update) | async-done | bytes 8388624 | tf_op jit(solution)/shard_map/all_gather | solution.py:20
  264.5 11.7 %cholesky.248 = f32[128,128]{1,0:T(8,128)S(1)} custom-call(f32[128,128]{1,0:T(8,128)S(1)} %cholesky.349), custom_call_target="Cholesky" | custom-call | tf_op jit(solution)/shard_map/jit(cholesky)/cholesky | solution.py:43
  276.3 9.8 %custom-call.35 = f32[1,128,128]{1,2,0:T(8,128)S(1)} custom-call(f32[1,128,128]{2,1,0:T(8,128)S(1)} %get-tuple-element.166), custom_call_target="InvertDiagBlocksLowerTriangular" | custom-call | tf_op jit(solution)/shard_map/jit(cholesky)/cholesky | solution.py:43
  286.6 11.7 %cholesky.265 = f32[128,128]{1,0:T(8,128)S(1)} custom-call(f32[128,128]{1,0:T(8,128)S(1)} %convolution_subtract_fusion.2), custom_call_target="Cholesky" | custom-call | tf_op jit(solution)/shard_map/jit(cholesky)/cholesky | solution.py:43
  300.9 4.2 while.29
  305.1 19.7 %custom-call.36 = f32[2,128,128]{1,2,0:T(8,128)S(1)} custom-call(f32[2,128,128]{2,1,0:T(8,128)S(1)} %get-tuple-element.90), custom_call_target="InvertDiagBlocksLowerTriangular" | custom-call | tf_op jit(solution)/shard_map/jit(_solve_triangular)/triangular_solve/custom-call.1 | solution.py:45
  326.1 6.2 fusion.5
  333.0 24.5 %scatter_custom_fusion.2 = f32[64,8192]{0,1:T(8,128)} fusion(s32[4096]{0:T(1024)S(1)} %bitcast.225, f32[4096,64]{1,0:T(8,128)S(1)} %copy.47, f32[]{:T(128)} %constant.212.clone.1), kind=kCustom, calls=%fused_computation.26 | custom fusion | flops 262144 | bytes 2097156 | tf_op jit(solution)/shard_map/scatter-add | solution.py:71
  360.3 5.5 scatter_custom_fusion.3
  368.9 47.2 %collective-permute-done.1 = f32[64,8192]{1,0:T(8,128)} collective-permute-done((f32[64,8192]{1,0:T(8,128)S(1)}, f32[64,8192]{1,0:T(8,128)}, u32[]{:S(2)}, u32[]{:S(2)}) %collective-permute-start.1) | collective-permute-done | bytes 2097184 | tf_op jit(solution)/shard_map/ppermute | solution.py:15
  421.4 68.1 %all-gather.9.cloned.1.call-done = f32[8192,256]{1,0:T(8,128)} async-done(((f32[64,256]{1,0:T(8,128)}), f32[8192,256]{1,0:T(8,128)}) %all-gather.9.cloned.1.call-update) | async-done | bytes 8388624 | tf_op jit(solution)/shard_map/all_gather | solution.py:20
  491.6 11.7 %cholesky.282 = f32[128,128]{1,0:T(8,128)S(1)} custom-call(f32[128,128]{1,0:T(8,128)S(1)} %cholesky.352), custom_call_target="Cholesky" | custom-call | tf_op jit(solution)/shard_map/jit(cholesky)/cholesky | solution.py:43
  503.4 9.8 %custom-call.39 = f32[1,128,128]{1,2,0:T(8,128)S(1)} custom-call(f32[1,128,128]{2,1,0:T(8,128)S(1)} %get-tuple-element.162), custom_call_target="InvertDiagBlocksLowerTriangular" | custom-call | tf_op jit(solution)/shard_map/jit(cholesky)/cholesky | solution.py:43
  513.7 11.7 %cholesky.299 = f32[128,128]{1,0:T(8,128)S(1)} custom-call(f32[128,128]{1,0:T(8,128)S(1)} %convolution_subtract_fusion.1), custom_call_target="Cholesky" | custom-call | tf_op jit(solution)/shard_map/jit(cholesky)/cholesky | solution.py:43
  528.0 4.0 while.30
  532.0 19.8 %custom-call.40 = f32[2,128,128]{1,2,0:T(8,128)S(1)} custom-call(f32[2,128,128]{2,1,0:T(8,128)S(1)} %get-tuple-element.93), custom_call_target="InvertDiagBlocksLowerTriangular" | custom-call | tf_op jit(solution)/shard_map/jit(_solve_triangular)/triangular_solve/custom-call.1 | solution.py:45
  553.2 11.9 %fusion = f32[64,8192]{1,0:T(8,128)S(1)} fusion(f32[64,8192]{1,0:T(8,128)} %copy-done, f32[8192,256]{1,0:T(8,128)} %all-gather.9.cloned.1.call-done, pred[8192]{0:T(1024)(128)(4,1)S(1)} %fusion.79, pred[64]{0:T(512)(128)(4,1)S(1)} %compare_or_fusion.2, f32[128,64]{0,1:T(8,128)S(1)} %fusion.61, f32[128,64]{0,1:T(8,128)S(1)} %fusion.59), kind=kOutput, calls=%fused_computation.14 | convolution fusion | flops 1612201984 | bytes 12656704 | tf_op jit(solution)/shard_map/rb,nb->rn/dot_general | solution.py:47
  567.3 65.7 %all-gather.11.cloned.1.call-done = f32[8192,256]{1,0:T(8,128)} async-done(((f32[64,256]{1,0:T(8,128)}), f32[8192,256]{1,0:T(8,128)}) %all-gather.11.cloned.1.call-update) | async-done | bytes 8388624 | tf_op jit(solution)/shard_map/all_gather | solution.py:20
  635.1 11.7 %cholesky.316 = f32[128,128]{1,0:T(8,128)S(1)} custom-call(f32[128,128]{1,0:T(8,128)S(1)} %cholesky.355), custom_call_target="Cholesky" | custom-call | tf_op jit(solution)/shard_map/jit(cholesky)/cholesky | solution.py:43
  646.9 10.0 %custom-call.43 = f32[1,128,128]{1,2,0:T(8,128)S(1)} custom-call(f32[1,128,128]{2,1,0:T(8,128)S(1)} %get-tuple-element.158), custom_call_target="InvertDiagBlocksLowerTriangular" | custom-call | tf_op jit(solution)/shard_map/jit(cholesky)/cholesky | solution.py:43
  657.4 11.7 %cholesky.333 = f32[128,128]{1,0:T(8,128)S(1)} custom-call(f32[128,128]{1,0:T(8,128)S(1)} %convolution_subtract_fusion), custom_call_target="Cholesky" | custom-call | tf_op jit(solution)/shard_map/jit(cholesky)/cholesky | solution.py:43
  671.8 4.0 while.31
  675.8 19.9 %custom-call.44 = f32[2,128,128]{1,2,0:T(8,128)S(1)} custom-call(f32[2,128,128]{2,1,0:T(8,128)S(1)} %get-tuple-element.96), custom_call_target="InvertDiagBlocksLowerTriangular" | custom-call | tf_op jit(solution)/shard_map/jit(_solve_triangular)/triangular_solve/custom-call.1 | solution.py:45
  697.8 12.8 %fusion.2 = f32[64,8192]{1,0:T(8,128)} fusion(f32[64,8192]{1,0:T(8,128)S(1)} %fusion, f32[8192,256]{1,0:T(8,128)} %all-gather.11.cloned.1.call-done, pred[8192]{0:T(1024)(128)(4,1)S(1)} %fusion.78, pred[64]{0:T(512)(128)(4,1)S(1)} %get-tuple-element.181, pred[64]{0:T(512)(128)(4,1)S(1)} %get-tuple-element.182, f32[128,64]{0,1:T(8,128)S(1)} %fusion.65, ...), kind=kOutput, calls=%fused_computation.16 | convolution fusion | flops 1613250560 | bytes 12656768 | tf_op jit(solution)/shard_map/rb,nb->rn/dot_general | solution.py:47
  (151 shorter events, 64.2 us)
Async XLA Ops:
  7.2 77.6 %all-gather.5.cloned.1.call-start = ((), (), s32[]{:S(2)}) async-start(), calls=%async_computation | async-start | bytes 8454144 | tf_op jit(solution)/shard_map/all_gather | solution.py:20
  8.7 253.7 %all-gather.7.cloned.1.call-start = ((), (), s32[]{:S(2)}) async-start(), calls=%async_computation.1 | async-start | bytes 8454144 | tf_op jit(solution)/shard_map/all_gather | solution.py:20
  85.9 62.2 %copy-start.1 = (f32[64,2048]{1,0:T(8,128)S(1)}, f32[64,2048]{1,0:T(8,128)}, u32[]{:S(2)}) copy-start(f32[64,2048]{1,0:T(8,128)} %param.10) | copy-start | bytes 1572868
  167.2 24.6 %collective-permute-start = (f32[64,4096]{1,0:T(8,128)S(1)}, f32[64,4096]{1,0:T(8,128)}, u32[]{:S(2)}, u32[]{:S(2)}) collective-permute-start(f32[64,4096]{1,0:T(8,128)S(1)} %constant_dynamic-slice_fusion.6), channel_id=1, source_target_pairs={{0,32},{1,33},{2,34},{3,35},{4,36},{5,37},{6,38},{7,39},{8,40},{9,... | collective-permute-start | bytes 3145736 | tf_op jit(solution)/shard_map/ppermute | solution.py:15
  167.3 27.4 %copy-start.2 = (s32[2,4096]{1,0:T(2,128)S(1)}, s32[2,4096]{1,0:T(2,128)}, u32[]{:S(2)}) copy-start(s32[2,4096]{1,0:T(2,128)} %param.14) | copy-start | bytes 98308
  194.2 295.3 %all-gather.9.cloned.1.call-start = ((), (), s32[]{:S(2)}) async-start(), calls=%async_computation.2 | async-start | bytes 8454144 | tf_op jit(solution)/shard_map/all_gather | solution.py:20
  367.6 48.6 %collective-permute-start.1 = (f32[64,8192]{1,0:T(8,128)S(1)}, f32[64,8192]{1,0:T(8,128)}, u32[]{:S(2)}, u32[]{:S(2)}) collective-permute-start(f32[64,8192]{1,0:T(8,128)S(1)} %constant_dynamic-slice_fusion.4), channel_id=1, source_target_pairs={{0,64},{1,65},{2,66},{3,67},{4,68},{5,69},{6,70},{7,71},{8,72},{9,... | collective-permute-start | bytes 6291464 | tf_op jit(solution)/shard_map/ppermute | solution.py:15
  419.3 1.3 copy-start
  421.3 211.7 %all-gather.11.cloned.1.call-start = ((), (), s32[]{:S(2)}) async-start(), calls=%async_computation.3 | async-start | bytes 8454144 | tf_op jit(solution)/shard_map/all_gather | solution.py:20
Sparse Core Ops, SparseCore 0:
  11.5 73.2 all-gather.4
  194.3 67.9 all-gather.6
  421.4 67.9 all-gather.8
  565.9 67.1 all-gather.10
where the time goes:
time: 726 us; the launch traced here: 718 us
  waiting for transfers between devices  347 us (48%)
  other arithmetic  274 us (38%)
  matrix products  41.6 us (6%)
  local copies, waits for them, and re-layouts  31.3 us (4%)
  between operations  20.3 us (3%)
    all_gather x4, waiting for transfers between devices, share_panel(): everything = lax.all_gather(own_cols, 'cube', axis=0, tiled=True)  276 us
    another operation x27, other arithmetic, eliminate(): lower_tri = jnp.linalg.cholesky(whole_panel[col_low:col_high])  138 us
    another operation x9, other arithmetic, eliminate(): jax.scipy.linalg.solve_triangular(lower_tri, own_cols.T, lower=True)  79.2 us
    ppermute x2, waiting for transfers between devices, from_partner(): return lax.ppermute(value, axis, pairs)  71.7 us
    scatter-add x2, other arithmetic, extend_add(): jnp.zeros((row_count, 2 * order), jnp.float32).at[:, own_map].add(masked)  36.5 us
    dot_general x4, matrix products, eliminate(): jnp.einsum('rb,nb->rn', weights, whole_panel, precision=lax.Precision.HIG...  34.6 us
    another operation x29, local copies, waits for them, and re-layouts, eliminate(): jax.scipy.linalg.solve_triangular(lower_tri, own_cols.T, lower=True)  15.9 us
  transfers between devices with their start and end apart: 6, of which 6 were waited for; matrix products, arithmetic and copies ran while one was open for 0% of the time, Pallas kernels for 0%

commit v1 on v0

v1 whole, which is shorter than its diff:
```python
import jax
import jax.numpy as jnp
from jax import lax
from jax.experimental import pallas as pl
from jax.experimental.pallas import tpu as pltpu
from jax.sharding import PartitionSpec as P

F32 = jnp.float32
BF16 = jnp.bfloat16
HI = lax.Precision.HIGHEST
MESH = pl.DeviceIdType.MESH
NN = ((1,), (0,))
NT = ((1,), (1,))
TILE = 256
MAX_COPIES = 192


def dot32(a, b, dims=NN):
    return lax.dot_general(a, b, (dims, ((), ())), precision=HI, preferred_element_type=F32)


def dot16(a, b, dims=NN):
    return lax.dot_general(a, b, (dims, ((), ())), preferred_element_type=F32)


def split(a):
    high = a.astype(BF16)
    return high, (a - high.astype(F32)).astype(BF16)


def bcast_row(v, j):
    return jnp.broadcast_to(v[j : j + 1, :], (8, 128))


def bcast_lane(v, j):
    return jnp.broadcast_to(v[:, j : j + 1], (8, 128))


def factor_tiles(tiles, tick):
    count = len(tiles)
    sub = lax.broadcasted_iota(jnp.int32, (8, 128), 0)
    tiles = [list(t) for t in tiles]
    outs = [[] for _ in range(count)]
    for r in range(8):
        cols = [[[bcast_lane(t[i], 8 * r + j) for j in range(8)] for i in range(r, 8)] for t in tiles]
        inv = [[None] * 8 for _ in range(count)]
        diag = [jnp.zeros((8, 128), F32) for _ in range(count)]
        for j in range(8):
            for q in range(count):
                b = cols[q]
                p = bcast_row(b[0][j], j)
                t = 1.0 / p
                inv[q][j] = t
                diag[q] = jnp.where(sub == j, p, diag[q])
                for m in range(j + 1, 8):
                    s = bcast_row(b[0][m], j) * t
                    for i in range(8 - r):
                        b[i][m] = b[i][m] - b[i][j] * s
                piv = bcast_row(tiles[q][r], j) * t
                below = jnp.where(sub > j, b[0][j], 0.0)
                tiles[q][r] = tiles[q][r] - below * piv
        for q in range(count):
            v = tiles[q][r]
            for j in range(8):
                piv = bcast_row(v, j) * inv[q][j]
                for i in range(r + 1, 8):
                    tiles[q][i] = tiles[q][i] - cols[q][i - r][j] * piv
            outs[q].append(v * lax.rsqrt(diag[q]))
        tick()
    return outs


def inverse_factor(a_refs, b_refs, t_refs, tick):
    count = len(a_refs)
    eye = lax.broadcasted_iota(jnp.int32, (64, 64), 0) == lax.broadcasted_iota(jnp.int32, (64, 64), 1)
    eye = eye.astype(F32)
    for q in range(count):
        b_refs[q][...] = jnp.zeros((256, 256), F32)
    for k in range(4):
        lo, hi = 64 * k, 64 * k + 64
        tiles = []
        for q in range(count):
            t_refs[q][:, 0:64] = a_refs[q][lo:hi, lo:hi]
            t_refs[q][:, 64:128] = eye
            tiles.append([t_refs[q][8 * i : 8 * i + 8, :] for i in range(8)])
        outs = factor_tiles(tiles, tick)
        for q in range(count):
            for i in range(8):
                t_refs[q][8 * i : 8 * i + 8, :] = outs[q][i]
            g = t_refs[q][:, 64:128]
            if k > 0:
                b_refs[q][lo:hi, 0:lo] = dot32(g, b_refs[q][lo:hi, 0:lo])
            b_refs[q][lo:hi, lo:hi] = g
            if k < 3:
                low = dot32(a_refs[q][hi:, lo:hi], g, NT)
                a_refs[q][hi:, hi:] = a_refs[q][hi:, hi:] - dot32(low, low, NT)
                b_refs[q][hi:, 0:hi] = b_refs[q][hi:, 0:hi] - dot32(low, b_refs[q][lo:hi, 0:hi])
        tick()


def kernel(g_ref, c_ref, r_ref, gm_ref, cm_ref, gf_ref, cf_ref, rf_ref, out_ref,
           pan_g, pan_c, pan_1, pan_0, dia_g, dia_c, dia_0, mat, inv, tile, c_acc,
           ug_send, ug_recv, uc_send, uc_relay, uc_recv, one_send, one_recv,
           send_sems, recv_sems, local_sems):
    me = lax.axis_index("cube")
    core = lax.rem(me, 2)
    y = lax.rem(me // 2, 4)
    z = lax.rem(me // 8, 4)
    x = me // 32
    x2 = lax.rem(x, 2)

    def at(xx, zz, yy):
        return ((lax.rem(xx, 4) * 4 + lax.rem(zz, 4)) * 4 + lax.rem(yy, 4)) * 2 + core

    other_core = me + 1 - 2 * core
    x_pair = me + 32 * (1 - 2 * x2)
    x_far = at(x + 2, z, y)

    used = [0]
    pending = []

    def new_sem(n=1):
        used[0] += n
        assert used[0] <= MAX_COPIES
        return used[0] - n

    def guarded(cond, fn):
        if cond is None:
            fn()
        else:
            pl.when(cond)(fn)

    def send(ref, dst, device, index, recv_index=None, cond=None):
        copy = pltpu.make_async_remote_copy(
            src_ref=ref, dst_ref=dst, send_sem=send_sems.at[index],
            recv_sem=recv_sems.at[index if recv_index is None else recv_index],
            device_id=(device,), device_id_type=MESH)
        guarded(cond, copy.start)
        pending.append((copy, cond))

    def arrived(ref, recv_index, cond=None):
        copy = pltpu.make_async_remote_copy(
            src_ref=ref, dst_ref=ref, send_sem=send_sems.at[0], recv_sem=recv_sems.at[recv_index],
            device_id=(other_core,), device_id_type=MESH)
        guarded(cond, copy.wait_recv)


    def gather_steps(buf, xs):
        xi = {4: x, 2: x2, 1: 0}[xs]

        def block(xx, rows=slice(None)):
            return buf.at[xx, z, y, core, rows]

        def part(half, phase, coord, rows=slice(None), cc=None):
            cc = core if cc is None else cc
            cols = slice(128 * half, 128 * half + 128)
            coord = lax.rem(coord, 4)
            if half == 0:
                if phase == 0:
                    return buf.at[:, coord, y, cc, rows, cols]
                return buf.at[:, :, coord, cc, rows, cols]
            if phase == 0:
                return buf.at[:, z, coord, cc, rows, cols]
            return buf.at[:, coord, :, cc, rows, cols]

        def axis_of(half, phase):
            return "zy"[(half + phase) % 2]

        def ends(half, phase):
            if axis_of(half, phase) == "z":
                return z, at(x, z + 1, y), at(x, z + 3, y)
            return y, at(x, z, y + 1), at(x, z, y + 3)

        top, bottom = slice(0, 32), slice(32, 64)
        sx = new_sem(4)
        if xs == 4:
            send(block(x), block(x), at(x + 1, z, y), sx)
            send(block(x), block(x), at(x + 3, z, y), sx + 1)
            yield
            xm, xp, xo = lax.rem(x + 3, 4), lax.rem(x + 1, 4), lax.rem(x + 2, 4)
            arrived(block(xm), sx)
            send(block(xm, top), block(xm, top), at(x + 1, z, y), sx + 2)
            arrived(block(xp), sx + 1)
            send(block(xp, bottom), block(xp, bottom), at(x + 3, z, y), sx + 3)
            yield
            arrived(block(xo, top), sx + 2)
            arrived(block(xo, bottom), sx + 3)
        elif xs == 2:
            send(block(x2), block(x2), x_pair, sx)
            yield
            arrived(block(1 - x2), sx)
        dd = new_sem(8)
        for phase in range(2):
            s = new_sem(8)
            for h in range(2):
                a, plus, minus = ends(h, phase)
                send(part(h, phase, a), part(h, phase, a), plus, s + 4 * h)
                send(part(h, phase, a), part(h, phase, a), minus, s + 4 * h + 1)
                if phase == 1:
                    send(part(h, 1, a), part(h, 1, a), other_core, dd + 4 * h)
            yield
            for h in range(2):
                a, plus, minus = ends(h, phase)
                arrived(part(h, phase, a + 3), s + 4 * h)
                send(part(h, phase, a + 3, top), part(h, phase, a + 3, top), plus, s + 4 * h + 2)
                arrived(part(h, phase, a + 1), s + 4 * h + 1)
                send(part(h, phase, a + 1, bottom), part(h, phase, a + 1, bottom), minus, s + 4 * h + 3)
                if phase == 1:
                    send(part(h, 1, a + 3), part(h, 1, a + 3), other_core, dd + 4 * h + 1)
                    send(part(h, 1, a + 1), part(h, 1, a + 1), other_core, dd + 4 * h + 2)
            yield
            for h in range(2):
                a, plus, minus = ends(h, phase)
                arrived(part(h, phase, a + 2, top), s + 4 * h + 2)
                arrived(part(h, phase, a + 2, bottom), s + 4 * h + 3)
                if phase == 1:
                    send(part(h, 1, a + 2), part(h, 1, a + 2), other_core, dd + 4 * h + 3)
        yield
        for h in range(2):
            a, plus, minus = ends(h, 1)
            for k, step in enumerate((0, 3, 1, 2)):
                arrived(part(h, 1, a + step, cc=1 - core), dd + 4 * h + k)


    def spread_steps(buf, x_mode, zs, ys):
        yi = jnp.where(y == ys + 1, 1, 0)
        in_y = (y == ys) | (y == ys + 1)
        slot = buf.at[yi, core]
        if x_mode is not None:
            sx = new_sem(3)
            own = in_y & (z == zs)
            if x_mode == "pair":
                send(slot, slot, x_pair, sx, cond=own & (x2 == 1))
                yield
                arrived(slot, sx, own & (x2 == 0))
            else:
                src = own & (x == 3)
                send(slot, slot, at(0, z, y), sx, sx, src)
                send(slot, slot, at(2, z, y), sx + 1, sx, src)
                send(slot, slot, at(1, z, y), sx + 2, sx, src)
                yield
                arrived(slot, sx, own & (x != 3))
        sz = new_sem(3)
        src = in_y & (z == zs)
        for k, step in enumerate((1, 3, 2)):
            send(slot, slot, at(x, zs + step, y), sz + k, sz, src)
        yield
        arrived(slot, sz, in_y & (z != zs))
        sy = new_sem(6)
        for k, step in enumerate((1, 3, 2)):
            send(slot, slot, at(x, z, y + step), sy + 2 + k, sy + yi, in_y)
        yield
        for k in range(2):
            arrived(buf.at[k, core], sy + k, y != ys + k)
        sd = new_sem(1)
        send(buf.at[:, core], buf.at[:, core], other_core, sd)
        yield
        arrived(buf.at[:, 1 - core], sd)

    def finish(gen):
        for _ in gen:
            pass

    def step(*gens):
        for gen in gens:
            next(gen, None)

    in_g = (z == 3) & (y < 2)
    in_c = in_g & (x2 == 1)
    yi01 = jnp.where(y == 1, 1, 0)
    starts = [
        (g_ref.at[:, 1536:1792], pan_g.at[0, z, y, core], None),
        (c_ref.at[:, 3584:3840], pan_c.at[x2, z, y, core], None),
        (r_ref.at[:, 7680:7936], pan_1.at[x, z, y, core], None),
        (g_ref.at[:, 1536:1792], dia_g.at[yi01, core], in_g),
        (c_ref.at[:, 3584:3840], dia_c.at[yi01, core], in_c),
    ]
    copies = [(pltpu.make_async_copy(a, b, local_sems.at[i]), cond) for i, (a, b, cond) in enumerate(starts)]
    for copy, cond in copies:
        guarded(cond, copy.start)

    barrier = pltpu.get_barrier_semaphore()
    peers = [at(x + k, z, y) for k in (1, 2, 3)] + [at(x, z + k, y) for k in (1, 2, 3)]
    peers += [at(x, z, y + k) for k in (1, 2, 3)] + [other_core]
    for peer in peers:
        pl.semaphore_signal(barrier, inc=1, device_id=(peer,), device_id_type=MESH)
    c_acc[...] = c_ref[...]
    for copy, cond in copies:
        guarded(cond, copy.wait)
    pl.semaphore_wait(barrier, len(peers))

    spread_g = spread_steps(dia_g, None, 3, 0)
    spread_c = spread_steps(dia_c, "pair", 3, 0)
    gather_g = gather_steps(pan_g, 1)
    gather_c = gather_steps(pan_c, 2)
    gather_1 = gather_steps(pan_1, 4)
    step(spread_c, spread_g, gather_c, gather_g, gather_1)
    step(spread_c, spread_g, gather_c, gather_g, gather_1)
    step(spread_c, spread_g)
    step(spread_c, spread_g)
    finish(spread_g)
    finish(spread_c)

    queue = [gather_g, gather_c, gather_1, gather_g, gather_c, gather_1, gather_g, gather_c, gather_g, gather_c,
             gather_1, gather_g, gather_c, gather_1]
    ticks = [0]

    def pump(every):
        def tick():
            ticks[0] += 1
            if ticks[0] % every == 0 and queue:
                step(queue.pop(0))
        return tick

    mat[0] = dia_g[...].reshape(256, 256)
    mat[1] = dia_c[...].reshape(256, 256)
    inverse_factor([mat.at[0], mat.at[1]], [inv.at[0], inv.at[1]], [tile.at[0], tile.at[1]], pump(2))

    low_g = dot32(g_ref[:, 1536:1792], inv[0], NT)
    gf_ref[...] = low_g
    wg_hi, wg_lo = split(dot32(low_g, inv[0]))
    wg_both = jnp.concatenate([wg_hi, wg_lo], 0)
    low_c = dot32(c_ref[:, 3584:3840], inv[1], NT)
    cf_ref[...] = low_c
    wc_hi, wc_lo = split(dot32(low_c, inv[1]))
    wc_both = jnp.concatenate([wc_hi, wc_lo], 0)

    def times_panel(both, high, panel):
        p_hi, p_lo = split(panel)
        prod = dot16(both, p_hi, NT)
        return prod[:64] + prod[64:] + dot16(high, p_lo, NT)

    def rows_of(buf, n):
        xx = n // 8
        zz = lax.rem(n // 2, 4) if not isinstance(n, int) else n // 2 % 4
        yy = 2 * (n % 2) if isinstance(n, int) else pl.multiple_of(2 * lax.rem(n, 2), 2)
        return buf[xx, zz, pl.ds(yy, 2)].reshape(256, 256)

    def lanes(n):
        return pl.ds(n * 256 if isinstance(n, int) else pl.multiple_of(n * 256, 256), 256)

    def map_row(map_ref, front, where):
        rows = map_ref[:, where]
        row = rows[0:1]
        for k in range(1, rows.shape[0]):
            row = jnp.where(front == k, rows[k : k + 1], row)
        return row

    def row_pick(map_ref, front, blk, base, keep):
        pair = map_row(map_ref, front, pl.ds(pl.multiple_of(128 * (blk // 2), 128), 128))
        mine = jnp.where(lax.rem(blk, 2) == 0, pair[:, 0:64], pair[:, 64:128])
        want = base + lax.broadcasted_iota(jnp.int32, (64, 64), 0)
        return jnp.where((mine == want) & keep, 1.0, 0.0).astype(BF16)

    def picked(pick, block):
        hi, lo = split(block)
        both = dot16(pick, jnp.concatenate([hi, lo], 1)).astype(BF16)
        return jnp.concatenate([both[:, 0:256], both[:, 256:512]], 0)

    def expand(map_ref, fronts, picks, blocks, n, base):
        lhs = jnp.concatenate([picked(p, b) for p, b in zip(picks, blocks)], 1)
        maps = [map_row(map_ref, f, lanes(n)) for f in fronts]
        where_to = jnp.concatenate(maps, 1)
        out = []
        for start in (0, base):
            want = 256 * n + start + lax.broadcasted_iota(jnp.int32, (256, 512), 0)
            hot = jnp.where(where_to == want, 1.0, 0.0).astype(BF16)
            prod = dot16(lhs, hot, NT)
            out.append(prod[:64] + prod[64:])
        return out

    def g_rows(n):
        return g_ref[:, lanes(n)] - times_panel(wg_both, wg_hi, rows_of(pan_g, n))

    finish(gather_g)
    one_send[0] = g_rows(5)
    s_one = new_sem(1)
    send(one_send.at[0], one_recv.at[0], x_pair, s_one)
    g_slots = (0, 1, 2, 3, 4, 7)
    for i, n in enumerate(g_slots):
        ug_send[i] = g_rows(n)
    s_g = new_sem(1)
    send(ug_send, ug_recv, x_pair, s_g)
    blk_g = lax.rem(me, 32)
    keep_g = (blk_g < 24) | (blk_g >= 28)
    base_g = 64 * lax.rem(me, 64)
    fronts_g = (x, x + 1 - 2 * x2)
    picks_g = [row_pick(gm_ref, f, blk_g, base_g, keep_g) for f in fronts_g]

    def add_g(n, own, other):
        lo, hi = expand(gm_ref, fronts_g, picks_g, [own, other], n, 2048)
        c_acc[:, lanes(n)] += lo
        c_acc[:, lanes(n + 8)] += hi

    arrived(one_recv.at[0], s_one)
    add_g(5, one_send[0], one_recv[0])

    def c_rows(n):
        return c_acc[:, lanes(n)] - times_panel(wc_both, wc_hi, rows_of(pan_c, n))

    finish(gather_c)
    one_send[1] = c_rows(13)
    s_one = new_sem(1)
    send(one_send.at[1], one_recv.at[1], x_far, s_one)
    while queue:
        step(queue.pop(0))
    blk_c = lax.rem(me, 64)
    keep_c = (blk_c < 56) | (blk_c >= 60)
    fronts_c = (x // 2, 1 - x // 2)
    picks_c = [row_pick(cm_ref, f, blk_c, 64 * me, keep_c) for f in fronts_c]

    arrived(one_recv.at[1], s_one)
    lo, hi = expand(cm_ref, fronts_c, picks_c, [one_send[1], one_recv[1]], 13, 4096)
    out_ref[:, 3328:3584] = r_ref[:, 3328:3584] + lo
    own_0 = r_ref[:, 7424:7680] + hi
    pan_0[x, z, y, core] = own_0
    in_0 = (x == 3) & (z == 2) & (y >= 2)

    @pl.when(in_0)
    def _():
        dia_0[jnp.where(y == 3, 1, 0), core] = own_0

    spread_0 = spread_steps(dia_0, "root", 2, 2)
    gather_0 = gather_steps(pan_0, 4)
    step(spread_0, gather_0)
    arrived(ug_recv, s_g)
    for i, n in enumerate(g_slots):
        add_g(n, ug_send[i], ug_recv[i])
        if i % 2 == 1:
            step(spread_0)

    def c_group(s):
        return jnp.where(s == 13, 15, s)

    def fill(s, _):
        uc_send[s] = c_rows(c_group(s))
        return 0

    s_c = new_sem(4)
    first, second = pl.ds(0, 7), pl.ds(7, 7)
    lax.fori_loop(0, 7, fill, 0)
    send(uc_send.at[first], uc_relay.at[first], at(x + 1, z, y), s_c)
    lax.fori_loop(7, 14, fill, 0)
    send(uc_send.at[second], uc_relay.at[second], at(x + 3, z, y), s_c + 1)
    finish(spread_0)

    def relay():
        arrived(uc_relay.at[first], s_c)
        send(uc_relay.at[first], uc_recv.at[first], at(x + 1, z, y), s_c + 2)
        yield
        arrived(uc_relay.at[second], s_c + 1)
        send(uc_relay.at[second], uc_recv.at[second], at(x + 3, z, y), s_c + 3)
        yield

    relay_c = relay()
    queue = [gather_0, gather_0, gather_0, relay_c, gather_0, relay_c, gather_0, gather_1, gather_1]

    def pump0(every):
        def tick():
            ticks[0] += 1
            if ticks[0] % every == 0 and queue:
                step(queue.pop(0))
        return tick

    mat[0] = dia_0[...].reshape(256, 256)
    inverse_factor([mat.at[0]], [inv.at[0]], [tile.at[0]], pump0(4))
    finish(gather_1)
    inv_0 = inv[0]
    cross = pan_1[3, 2, 2:4].reshape(256, 256)
    low_x = dot32(inv_0, cross)
    mat[1] = pan_1[3, 3, 0:2].reshape(256, 256) - dot32(low_x, low_x, ((0,), (0,)))
    inverse_factor([mat.at[1]], [inv.at[1]], [tile.at[1]], pump0(2))
    inv_1 = inv[1]

    low_0 = dot32(own_0, inv_0, NT)
    rf_ref[:, 0:256] = low_0
    own_1 = r_ref[:, 7680:7936] - dot32(low_0, low_x)
    low_1 = dot32(own_1, inv_1, NT)
    rf_ref[:, 256:512] = jnp.where(in_0, 0.0, low_1)
    w_1 = dot32(low_1, inv_1)
    m_0 = dot32(low_0 - dot32(w_1, low_x, NT), inv_0)
    w_hi, w_lo = split(jnp.concatenate([m_0, w_1], 1))
    w_both = jnp.concatenate([w_hi, w_lo], 0)

    while queue:
        step(queue.pop(0))
    finish(relay_c)
    arrived(uc_recv.at[first], s_c + 2)
    arrived(uc_recv.at[second], s_c + 3)

    def add_c(s, _):
        n = c_group(s)
        lo, hi = expand(cm_ref, fronts_c, picks_c, [uc_send[s], uc_recv[s]], n, 4096)
        out_ref[:, lanes(n)] = r_ref[:, lanes(n)] + lo
        out_ref[:, lanes(n + 16)] = r_ref[:, lanes(n + 16)] + hi
        return 0

    lax.fori_loop(0, 14, add_c, 0)
    out_ref[:, 3584:3840] = r_ref[:, 3584:3840]
    finish(gather_0)

    row_kept = jnp.logical_not((x == 3) & (((z == 2) & (y >= 2)) | ((z == 3) & (y < 2))))

    def last(t, _):
        n = jnp.where(t >= 29, t + 2, t)
        panel = jnp.concatenate([rows_of(pan_0, n), rows_of(pan_1, n)], 1)
        res = out_ref[:, lanes(n)] - times_panel(w_both, w_hi, panel)
        out_ref[:, lanes(n)] = jnp.where(row_kept, res, 0.0)
        return 0

    lax.fori_loop(0, 30, last, 0)
    out_ref[:, 7424:7936] = jnp.zeros((64, 512), F32)

    for copy, cond in pending:
        guarded(cond, copy.wait_send)


def local(gfront, cfront, rfront, gmap, cmap):
    vmem = pl.BlockSpec(memory_space=pltpu.VMEM)
    block = (64, 256)
    return pl.pallas_call(
        kernel,
        out_shape=(
            jax.ShapeDtypeStruct((64, 256), F32),
            jax.ShapeDtypeStruct((64, 256), F32),
            jax.ShapeDtypeStruct((64, 512), F32),
            jax.ShapeDtypeStruct((64, 8192), F32),
        ),
        in_specs=[vmem] * 5,
        out_specs=(vmem,) * 4,
        scratch_shapes=[
            pltpu.VMEM((1, 4, 4, 2) + block, F32),
            pltpu.VMEM((2, 4, 4, 2) + block, F32),
            pltpu.VMEM((4, 4, 4, 2) + block, F32),
            pltpu.VMEM((4, 4, 4, 2) + block, F32),
            pltpu.VMEM((2, 2) + block, F32),
            pltpu.VMEM((2, 2) + block, F32),
            pltpu.VMEM((2, 2) + block, F32),
            pltpu.VMEM((2, 256, 256), F32),
            pltpu.VMEM((2, 256, 256), F32),
            pltpu.VMEM((2, 64, 128), F32),
            pltpu.VMEM((64, 4096), F32),
            pltpu.VMEM((6,) + block, F32),
            pltpu.VMEM((6,) + block, F32),
            pltpu.VMEM((14,) + block, F32),
            pltpu.VMEM((14,) + block, F32),
            pltpu.VMEM((14,) + block, F32),
            pltpu.VMEM((2,) + block, F32),
            pltpu.VMEM((2,) + block, F32),
            pltpu.SemaphoreType.DMA((MAX_COPIES,)),
            pltpu.SemaphoreType.DMA((MAX_COPIES,)),
            pltpu.SemaphoreType.DMA((8,)),
        ],
        compiler_params=pltpu.CompilerParams(
            collective_id=0, has_side_effects=True, vmem_limit_bytes=60 * 1024 * 1024
        ),
    )(gfront, cfront, rfront, gmap, cmap)


def solution(mesh):
    rows = P("cube", None)
    return jax.shard_map(
        local,
        mesh=mesh,
        in_specs=(rows, rows, rows, P(), P()),
        out_specs=(rows, rows, rows, rows),
        check_vma=False,
    )
```

time: 726 us -> 176 us (0.24)
  waiting for transfers between devices: 347 us -> 0 us
  other arithmetic: 274 us -> 0 us
  Pallas kernels: 0 us -> 167 us
  matrix products: 41.6 us -> 0 us
  local copies, waits for them, and re-layouts: 31.3 us -> 7.57 us
  between operations: 20.3 us -> 0.64 us
    all_gather x4 -> x0, waiting for transfers between devices: 276 us -> none  [share_panel(): everything = lax.all_gather(own_cols, 'cube', axis=0, tiled=True)]
    another operation x36 -> x0, other arithmetic: 217 us -> none  [the longest x27 138 us: eliminate(): lower_tri = jnp.linalg.cholesky(whole_panel[col_low:col_high])]
    pallas_call x0 -> x1, Pallas kernels: none -> 167 us  [local(): pl.pallas_call(kernel, out_shape=(jax.ShapeDtypeStruct((64, 256), F32), j...]
    ppermute x2 -> x0, waiting for transfers between devices: 71.7 us -> none  [from_partner(): return lax.ppermute(value, axis, pairs)]
    scatter-add x4 -> x0, other arithmetic: 44.4 us -> none  [the longest x2 36.5 us: extend_add(): jnp.zeros((row_count, 2 * order), jnp.float32).at[:, own_map].add(masked)]
    dot_general x4 -> x0, matrix products: 34.6 us -> none  [eliminate(): jnp.einsum('rb,nb->rn', weights, whole_panel, precision=lax.Precision.HIG...]
    another operation x37 -> x0, local copies, waits for them, and re-layouts: 16 us -> none  [the longest x29 15.9 us: eliminate(): jax.scipy.linalg.solve_triangular(lower_tri, own_cols.T, lower=True)]
  transfers between devices with their start and end apart: 6 -> 0, of which waited for: 6 -> 0; matrix products, arithmetic and copies ran while one was open for 0% -> 0% of each run, Pallas kernels for 0% -> 0%
where the time goes in v1:
time: 176 us; the launch traced here: 175 us
  Pallas kernels  167 us (95%)
  local copies, waits for them, and re-layouts  7.57 us (4%)
    pallas_call x1, Pallas kernels, local(): pl.pallas_call(kernel, out_shape=(jax.ShapeDtypeStruct((64, 256), F32), j...  167 us
    unnamed x4, local copies, waits for them, and re-layouts  7.57 us

profile of v1, /device:TPU:1, one launch (start us, length us, event | category | flops | bytes accessed | tf_op | source)
XLA Modules:
  0.0 174.7 jit_solution(14887592765021659192)
XLA Ops:
  0.6 166.5 %shard_map.84 = (f32[64,256]{1,0:T(8,128)}, f32[64,256]{1,0:T(8,128)}, f32[64,512]{1,0:T(8,128)}, f32[64,8192]{1,0:T(8,128)}) custom-call(f32[64,2048]{1,0:T(8,128)} %g_ref.1, f32[64,4096]{1,0:T(8,128)} %c_ref.1, f32[64,8192]{1,0:T(8,128)} %r_ref.1, s32[4,2048]{1,0:T(4,128)} %gm_ref.1, s32[2,4096]{1,0:T(2,128)} %cm_ref.1), custom_call_target="tpu_custom_call" | custom-call | tf_op jit(solution)/shard_map/pallas_call | solution.py:521
  167.2 1.5 copy.13
  168.6 1.5 copy.14
  170.1 1.6 copy.15
  171.7 3.1 %copy.16 = f32[64,8192]{1,0:T(8,128)} copy(f32[64,8192]{1,0:T(8,128)} %get-tuple-element.11) | data formatting | bytes 4194304

commit v2 on v1

--- a/solution.py
+++ b/solution.py
@@ -12,7 +12,7 @@
 NN = ((1,), (0,))
 NT = ((1,), (1,))
 TILE = 256
-MAX_COPIES = 192
+MAX_COPIES = 224
 
 
 def dot32(a, b, dims=NN):
@@ -70,10 +70,18 @@
     return outs
 
 
-def inverse_factor(a_refs, b_refs, t_refs, tick):
+def inverse_factor(a_refs, b_refs, t_refs, tick, extra=None):
     count = len(a_refs)
     eye = lax.broadcasted_iota(jnp.int32, (64, 64), 0) == lax.broadcasted_iota(jnp.int32, (64, 64), 1)
     eye = eye.astype(F32)
+    later = []
+
+    def both_ticks():
+        for _ in range(count):
+            if later:
+                later.pop(0)()
+        tick()
+
     for q in range(count):
         b_refs[q][...] = jnp.zeros((256, 256), F32)
     for k in range(4):
@@ -83,25 +91,61 @@
             t_refs[q][:, 0:64] = a_refs[q][lo:hi, lo:hi]
             t_refs[q][:, 64:128] = eye
             tiles.append([t_refs[q][8 * i : 8 * i + 8, :] for i in range(8)])
-        outs = factor_tiles(tiles, tick)
+        outs = factor_tiles(tiles, both_ticks)
+        while later:
+            later.pop(0)()
+        waiting = []
         for q in range(count):
             for i in range(8):
                 t_refs[q][8 * i : 8 * i + 8, :] = outs[q][i]
-            g = t_refs[q][:, 64:128]
-            if k > 0:
-                b_refs[q][lo:hi, 0:lo] = dot32(g, b_refs[q][lo:hi, 0:lo])
-            b_refs[q][lo:hi, lo:hi] = g
-            if k < 3:
-                low = dot32(a_refs[q][hi:, lo:hi], g, NT)
-                a_refs[q][hi:, hi:] = a_refs[q][hi:, hi:] - dot32(low, low, NT)
-                b_refs[q][hi:, 0:hi] = b_refs[q][hi:, 0:hi] - dot32(low, b_refs[q][lo:hi, 0:hi])
-        tick()
-
-
-def kernel(g_ref, c_ref, r_ref, gm_ref, cm_ref, gf_ref, cf_ref, rf_ref, out_ref,
-           pan_g, pan_c, pan_1, pan_0, dia_g, dia_c, dia_0, mat, inv, tile, c_acc,
+            waiting.append(rest_of_block(a_refs[q], b_refs[q], t_refs[q][:, 64:128], lo, hi))
+        later = [fn for group in zip(*waiting) for fn in group]
+        if extra is not None:
+            later += extra(k)
+    while later:
+        later.pop(0)()
+
+
+def rest_of_block(a, b, g, lo, hi):
+    end = hi + 64
+    if lo < 192:
+        low = dot32(a[hi:end, lo:hi], g, NT)
+        a[hi:end, hi:end] = a[hi:end, hi:end] - dot32(low, low, NT)
+    rest = []
+    keep = {}
+
+    def rest_low():
+        keep["low"] = dot32(a[end:, lo:hi], g, NT)
+        a[end:, hi:end] = a[end:, hi:end] - dot32(keep["low"], low, NT)
+
+    def rest_square():
+        a[end:, end:] = a[end:, end:] - dot32(keep["low"], keep["low"], NT)
+
+    def own_inverse():
+        if lo > 0:
+            b[lo:hi, 0:lo] = dot32(g, b[lo:hi, 0:lo])
+        b[lo:hi, lo:hi] = g
+
+    def next_inverse():
+        b[hi:end, 0:hi] = b[hi:end, 0:hi] - dot32(low, b[lo:hi, 0:hi])
+
+    def rest_inverse():
+        b[end:, 0:hi] = b[end:, 0:hi] - dot32(keep["low"], b[lo:hi, 0:hi])
+
+    if lo < 128:
+        rest += [rest_low, rest_square]
+    rest.append(own_inverse)
+    if lo < 192:
+        rest.append(next_inverse)
+    if lo < 128:
+        rest.append(rest_inverse)
+    return rest
+
+
+def kernel(g_hbm, c_hbm, r_hbm, gm_hbm, cm_hbm, gf_ref, cf_ref, rf_ref, out_hbm,
+           g_ref, out_ref, gm_ref, cm_ref, pan_g, pan_c, pan_1, pan_0, dia_g, dia_c, dia_0, mat, inv, tile, c_acc,
            ug_send, ug_recv, uc_send, uc_relay, uc_recv, one_send, one_recv,
-           send_sems, recv_sems, local_sems):
+           low_x, x_mat, own_1, m_own, send_sems, recv_sems, local_sems, out_sems):
     me = lax.axis_index("cube")
     core = lax.rem(me, 2)
     y = lax.rem(me // 2, 4)
@@ -240,18 +284,28 @@
                 send(slot, slot, at(1, z, y), sx + 2, sx, src)
                 yield
                 arrived(slot, sx, own & (x != 3))
-        sz = new_sem(3)
+        left, right = (slice(None), slice(0, 128)), (slice(None), slice(128, 256))
+        s1 = new_sem(8)
         src = in_y & (z == zs)
-        for k, step in enumerate((1, 3, 2)):
-            send(slot, slot, at(x, zs + step, y), sz + k, sz, src)
-        yield
-        arrived(slot, sz, in_y & (z != zs))
-        sy = new_sem(6)
-        for k, step in enumerate((1, 3, 2)):
-            send(slot, slot, at(x, z, y + step), sy + 2 + k, sy + yi, in_y)
-        yield
+        zline = z == zs
+        one = buf.at[(yi, core) + left]
+        two = buf.at[(yi, core) + right]
+        for k, inc in enumerate((1, 3, 2)):
+            send(one, one, at(x, zs + inc, y), s1 + k, s1, src)
+            send(two, two, at(x, zs, y + inc), s1 + 3 + k, s1 + 3 + yi, src)
+        yield
+        arrived(one, s1, in_y & (z != zs))
         for k in range(2):
-            arrived(buf.at[k, core], sy + k, y != ys + k)
+            arrived(buf.at[(k, core) + right], s1 + 3 + k, zline & (y != ys + k))
+        s2 = new_sem(8)
+        pair = buf.at[(slice(None), core) + right]
+        for k, inc in enumerate((1, 3, 2)):
+            send(one, one, at(x, z, y + inc), s2 + k, s2 + yi, in_y)
+            send(pair, pair, at(x, zs + inc, y), s2 + 3 + k, s2 + 3, zline)
+        yield
+        for k in range(2):
+            arrived(buf.at[(k, core) + left], s2 + k, y != ys + k)
+        arrived(pair, s2 + 3, z != zs)
         sd = new_sem(1)
         send(buf.at[:, core], buf.at[:, core], other_core, sd)
         yield
@@ -269,14 +323,19 @@
     in_c = in_g & (x2 == 1)
     yi01 = jnp.where(y == 1, 1, 0)
     starts = [
-        (g_ref.at[:, 1536:1792], pan_g.at[0, z, y, core], None),
-        (c_ref.at[:, 3584:3840], pan_c.at[x2, z, y, core], None),
-        (r_ref.at[:, 7680:7936], pan_1.at[x, z, y, core], None),
-        (g_ref.at[:, 1536:1792], dia_g.at[yi01, core], in_g),
-        (c_ref.at[:, 3584:3840], dia_c.at[yi01, core], in_c),
+        (g_hbm.at[:, 1536:1792], pan_g.at[0, z, y, core], None),
+        (c_hbm.at[:, 3584:3840], pan_c.at[x2, z, y, core], None),
+        (g_hbm.at[:, 1536:1792], dia_g.at[yi01, core], in_g),
+        (c_hbm.at[:, 3584:3840], dia_c.at[yi01, core], in_c),
+        (r_hbm.at[:, 7680:7936], pan_1.at[x, z, y, core], None),
+        (g_hbm, g_ref, None),
+        (gm_hbm, gm_ref, None),
+        (cm_hbm, cm_ref, None),
+        (c_hbm, c_acc, None),
+        (r_hbm, out_ref, None),
     ]
-    copies = [(pltpu.make_async_copy(a, b, local_sems.at[i]), cond) for i, (a, b, cond) in enumerate(starts)]
-    for copy, cond in copies:
+    loads = [(pltpu.make_async_copy(a, b, local_sems.at[i]), cond) for i, (a, b, cond) in enumerate(starts)]
+    for copy, cond in loads:
         guarded(cond, copy.start)
 
     barrier = pltpu.get_barrier_semaphore()
@@ -284,8 +343,7 @@
     peers += [at(x, z, y + k) for k in (1, 2, 3)] + [other_core]
     for peer in peers:
         pl.semaphore_signal(barrier, inc=1, device_id=(peer,), device_id_type=MESH)
-    c_acc[...] = c_ref[...]
-    for copy, cond in copies:
+    for copy, cond in loads[:4]:
         guarded(cond, copy.wait)
     pl.semaphore_wait(barrier, len(peers))
 
@@ -294,33 +352,39 @@
     gather_g = gather_steps(pan_g, 1)
     gather_c = gather_steps(pan_c, 2)
     gather_1 = gather_steps(pan_1, 4)
-    step(spread_c, spread_g, gather_c, gather_g, gather_1)
-    step(spread_c, spread_g, gather_c, gather_g, gather_1)
-    step(spread_c, spread_g)
-    step(spread_c, spread_g)
+    step(spread_c, spread_g, gather_c, gather_g)
+    step(spread_c, gather_c)
+    step(spread_g, gather_g)
+    step(spread_c, gather_c)
+    step(spread_g, spread_c, gather_g, gather_c)
     finish(spread_g)
     finish(spread_c)
 
-    queue = [gather_g, gather_c, gather_1, gather_g, gather_c, gather_1, gather_g, gather_c, gather_g, gather_c,
-             gather_1, gather_g, gather_c, gather_1]
-    ticks = [0]
-
-    def pump(every):
+    def timed(plan):
+        count = [0]
+
         def tick():
-            ticks[0] += 1
-            if ticks[0] % every == 0 and queue:
-                step(queue.pop(0))
+            count[0] += 1
+            for fn in plan.get(count[0], ()):
+                if callable(fn):
+                    fn()
+                else:
+                    step(fn)
         return tick
 
+    for copy, cond in loads[4:]:
+        copy.wait()
     mat[0] = dia_g[...].reshape(256, 256)
     mat[1] = dia_c[...].reshape(256, 256)
-    inverse_factor([mat.at[0], mat.at[1]], [inv.at[0], inv.at[1]], [tile.at[0], tile.at[1]], pump(2))
-
-    low_g = dot32(g_ref[:, 1536:1792], inv[0], NT)
+    inverse_factor([mat.at[0], mat.at[1]], [inv.at[0], inv.at[1]], [tile.at[0], tile.at[1]], timed({
+        2: [gather_1], 7: [gather_1], 10: [gather_g], 12: [gather_1], 15: [gather_c], 17: [gather_1],
+        20: [gather_g], 23: [gather_1], 28: [gather_c]}))
+
+    low_g = dot32(pan_g[0, z, y, core], inv[0], NT)
     gf_ref[...] = low_g
     wg_hi, wg_lo = split(dot32(low_g, inv[0]))
     wg_both = jnp.concatenate([wg_hi, wg_lo], 0)
-    low_c = dot32(c_ref[:, 3584:3840], inv[1], NT)
+    low_c = dot32(pan_c[x2, z, y, core], inv[1], NT)
     cf_ref[...] = low_c
     wc_hi, wc_lo = split(dot32(low_c, inv[1]))
     wc_both = jnp.concatenate([wc_hi, wc_lo], 0)
@@ -402,8 +466,7 @@
     one_send[1] = c_rows(13)
     s_one = new_sem(1)
     send(one_send.at[1], one_recv.at[1], x_far, s_one)
-    while queue:
-        step(queue.pop(0))
+    step(gather_1)
     blk_c = lax.rem(me, 64)
     keep_c = (blk_c < 56) | (blk_c >= 60)
     fronts_c = (x // 2, 1 - x // 2)
@@ -411,8 +474,8 @@
 
     arrived(one_recv.at[1], s_one)
     lo, hi = expand(cm_ref, fronts_c, picks_c, [one_send[1], one_recv[1]], 13, 4096)
-    out_ref[:, 3328:3584] = r_ref[:, 3328:3584] + lo
-    own_0 = r_ref[:, 7424:7680] + hi
+    out_ref[:, 3328:3584] += lo
+    own_0 = out_ref[:, 7424:7680] + hi
     pan_0[x, z, y, core] = own_0
     in_0 = (x == 3) & (z == 2) & (y >= 2)
 
@@ -423,83 +486,98 @@
     spread_0 = spread_steps(dia_0, "root", 2, 2)
     gather_0 = gather_steps(pan_0, 4)
     step(spread_0, gather_0)
+
+    def c_group(s):
+        return jnp.where(s == 13, 15, s) if not isinstance(s, int) else s + 2 * (s == 13)
+
+    def fill(s, _):
+        uc_send[s] = c_rows(c_group(s))
+        return 0
+
+    s_c = new_sem(4)
+    first, second = pl.ds(0, 7), pl.ds(7, 7)
+
+    def relay():
+        arrived(uc_relay.at[first], s_c)
+        send(uc_relay.at[first], uc_recv.at[first], at(x + 1, z, y), s_c + 2)
+        yield
+        arrived(uc_relay.at[second], s_c + 1)
+        send(uc_relay.at[second], uc_recv.at[second], at(x + 3, z, y), s_c + 3)
+        yield
+        arrived(uc_recv.at[first], s_c + 2)
+        yield
+        arrived(uc_recv.at[second], s_c + 3)
+        yield
+
+    def add_c(s):
+        n = c_group(s)
+        lo, hi = expand(cm_ref, fronts_c, picks_c, [uc_send[s], uc_recv[s]], n, 4096)
+        out_ref[:, lanes(n)] += lo
+        out_ref[:, lanes(n + 16)] += hi
+
     arrived(ug_recv, s_g)
     for i, n in enumerate(g_slots):
         add_g(n, ug_send[i], ug_recv[i])
-        if i % 2 == 1:
-            step(spread_0)
-
-    def c_group(s):
-        return jnp.where(s == 13, 15, s)
-
-    def fill(s, _):
-        uc_send[s] = c_rows(c_group(s))
-        return 0
-
-    s_c = new_sem(4)
-    first, second = pl.ds(0, 7), pl.ds(7, 7)
+        if i == 2:
+            step(spread_0, gather_0)
     lax.fori_loop(0, 7, fill, 0)
     send(uc_send.at[first], uc_relay.at[first], at(x + 1, z, y), s_c)
+    step(spread_0, gather_0, gather_1)
     lax.fori_loop(7, 14, fill, 0)
     send(uc_send.at[second], uc_relay.at[second], at(x + 3, z, y), s_c + 1)
+    step(spread_0)
+    step(gather_0)
     finish(spread_0)
-
-    def relay():
-        arrived(uc_relay.at[first], s_c)
-        send(uc_relay.at[first], uc_recv.at[first], at(x + 1, z, y), s_c + 2)
-        yield
-        arrived(uc_relay.at[second], s_c + 1)
-        send(uc_relay.at[second], uc_recv.at[second], at(x + 3, z, y), s_c + 3)
-        yield
-
+    finish(gather_1)
     relay_c = relay()
-    queue = [gather_0, gather_0, gather_0, relay_c, gather_0, relay_c, gather_0, gather_1, gather_1]
-
-    def pump0(every):
-        def tick():
-            ticks[0] += 1
-            if ticks[0] % every == 0 and queue:
-                step(queue.pop(0))
-        return tick
 
     mat[0] = dia_0[...].reshape(256, 256)
-    inverse_factor([mat.at[0]], [inv.at[0]], [tile.at[0]], pump0(4))
-    finish(gather_1)
-    inv_0 = inv[0]
-    cross = pan_1[3, 2, 2:4].reshape(256, 256)
-    low_x = dot32(inv_0, cross)
-    mat[1] = pan_1[3, 3, 0:2].reshape(256, 256) - dot32(low_x, low_x, ((0,), (0,)))
-    inverse_factor([mat.at[1]], [inv.at[1]], [tile.at[1]], pump0(2))
+    mat[1] = pan_1[3, 3, 0:2].reshape(256, 256)
+
+    def root_block(k):
+        def share():
+            hi = 64 * k + 64
+            cross = pan_1[3, 2, 2:4].reshape(256, 256)[0:hi]
+            low = dot32(inv[0, 64 * k : hi, 0:hi], cross)
+            low_x[64 * k : hi] = low
+            mat[1] -= dot32(low, low, ((0,), (0,)))
+        return [share]
+
+    inverse_factor([mat.at[0]], [inv.at[0]], [tile.at[0]], timed({
+        6: [gather_0], 18: [relay_c], 22: [relay_c], 30: [gather_0]}), root_block)
+
+    def own_low():
+        low = dot32(own_0, inv[0], NT)
+        rf_ref[:, 0:256] = low
+
+    def own_next():
+        low = rf_ref[:, 0:256]
+        own_1[...] = pan_1[x, z, y, core] - dot32(low, low_x[...])
+        m_own[...] = dot32(low, inv[0])
+
+    def cross_weight():
+        x_mat[...] = dot32(low_x[...], inv[0], ((0,), (0,)))
+
+    plan = {1: [own_low], 2: [own_next], 3: [cross_weight, relay_c], 14: [gather_0], 17: [relay_c]}
+    for k in range(7):
+        plan.setdefault(4 + 2 * k, []).append(lambda k=k: add_c(k))
+        plan.setdefault(18 + 2 * k, []).append(lambda k=k: add_c(7 + k))
+    inverse_factor([mat.at[1]], [inv.at[1]], [tile.at[1]], timed(plan))
     inv_1 = inv[1]
 
-    low_0 = dot32(own_0, inv_0, NT)
-    rf_ref[:, 0:256] = low_0
-    own_1 = r_ref[:, 7680:7936] - dot32(low_0, low_x)
-    low_1 = dot32(own_1, inv_1, NT)
+    low_1 = dot32(own_1[...], inv_1, NT)
     rf_ref[:, 256:512] = jnp.where(in_0, 0.0, low_1)
     w_1 = dot32(low_1, inv_1)
-    m_0 = dot32(low_0 - dot32(w_1, low_x, NT), inv_0)
+    m_0 = m_own[...] - dot32(w_1, x_mat[...])
     w_hi, w_lo = split(jnp.concatenate([m_0, w_1], 1))
     w_both = jnp.concatenate([w_hi, w_lo], 0)
 
-    while queue:
-        step(queue.pop(0))
     finish(relay_c)
-    arrived(uc_recv.at[first], s_c + 2)
-    arrived(uc_recv.at[second], s_c + 3)
-
-    def add_c(s, _):
-        n = c_group(s)
-        lo, hi = expand(cm_ref, fronts_c, picks_c, [uc_send[s], uc_recv[s]], n, 4096)
-        out_ref[:, lanes(n)] = r_ref[:, lanes(n)] + lo
-        out_ref[:, lanes(n + 16)] = r_ref[:, lanes(n + 16)] + hi
-        return 0
-
-    lax.fori_loop(0, 14, add_c, 0)
-    out_ref[:, 3584:3840] = r_ref[:, 3584:3840]
     finish(gather_0)
 
     row_kept = jnp.logical_not((x == 3) & (((z == 2) & (y >= 2)) | ((z == 3) & (y < 2))))
+
+    out_ref[:, 7424:7936] = jnp.zeros((64, 512), F32)
 
     def last(t, _):
         n = jnp.where(t >= 29, t + 2, t)
@@ -508,8 +586,15 @@
         out_ref[:, lanes(n)] = jnp.where(row_kept, res, 0.0)
         return 0
 
-    lax.fori_loop(0, 30, last, 0)
-    out_ref[:, 7424:7936] = jnp.zeros((64, 512), F32)
+    for part in range(5):
+        lax.fori_loop(6 * part, 6 * part + 6, last, 0)
+        first_n, last_n = 6 * part, (6 * part + 6 if part < 4 else 32)
+        where = slice(256 * first_n, 256 * last_n)
+        pltpu.make_async_copy(out_ref.at[:, where], out_hbm.at[:, where], out_sems.at[part]).start()
+    for part in range(5):
+        first_n, last_n = 6 * part, (6 * part + 6 if part < 4 else 32)
+        where = slice(256 * first_n, 256 * last_n)
+        pltpu.make_async_copy(out_ref.at[:, where], out_hbm.at[:, where], out_sems.at[part]).wait()
 
     for copy, cond in pending:
         guarded(cond, copy.wait_send)
@@ -517,8 +602,9 @@
 
 def local(gfront, cfront, rfront, gmap, cmap):
     vmem = pl.BlockSpec(memory_space=pltpu.VMEM)
+    hbm = pl.BlockSpec(memory_space=pl.ANY)
     block = (64, 256)
-    return pl.pallas_call(
+    parts = pl.pallas_call(
         kernel,
         out_shape=(
             jax.ShapeDtypeStruct((64, 256), F32),
@@ -526,9 +612,13 @@
             jax.ShapeDtypeStruct((64, 512), F32),
             jax.ShapeDtypeStruct((64, 8192), F32),
         ),
-        in_specs=[vmem] * 5,
-        out_specs=(vmem,) * 4,
+        in_specs=[hbm] * 5,
+        out_specs=(vmem, vmem, vmem, hbm),
         scratch_shapes=[
+            pltpu.VMEM((64, 2048), F32),
+            pltpu.VMEM((64, 8192), F32),
+            pltpu.VMEM((4, 2048), jnp.int32),
+            pltpu.VMEM((2, 4096), jnp.int32),
             pltpu.VMEM((1, 4, 4, 2) + block, F32),
             pltpu.VMEM((2, 4, 4, 2) + block, F32),
             pltpu.VMEM((4, 4, 4, 2) + block, F32),
@@ -547,14 +637,46 @@
             pltpu.VMEM((14,) + block, F32),
             pltpu.VMEM((2,) + block, F32),
             pltpu.VMEM((2,) + block, F32),
+            pltpu.VMEM((256, 256), F32),
+            pltpu.VMEM((256, 256), F32),
+            pltpu.VMEM((64, 256), F32),
+            pltpu.VMEM((64, 256), F32),
             pltpu.SemaphoreType.DMA((MAX_COPIES,)),
             pltpu.SemaphoreType.DMA((MAX_COPIES,)),
-            pltpu.SemaphoreType.DMA((8,)),
+            pltpu.SemaphoreType.DMA((10,)),
+            pltpu.SemaphoreType.DMA((5,)),
         ],
         compiler_params=pltpu.CompilerParams(
             collective_id=0, has_side_effects=True, vmem_limit_bytes=60 * 1024 * 1024
         ),
     )(gfront, cfront, rfront, gmap, cmap)
+
+
+    chunks = [(0, slice(0, 256)), (1, slice(0, 256)), (2, slice(0, 512))]
+    chunks += [(3, slice(2048 * k, 2048 * k + 2048)) for k in range(4)]
+
+    def write(*refs):
+        src, dst, buf, sems = refs[:4], refs[4:8], refs[8:12], refs[12]
+        reads = [pltpu.make_async_copy(src[a].at[:, w], buf[a].at[:, w], sems.at[0, k])
+                 for k, (a, w) in enumerate(chunks)]
+        writes = [pltpu.make_async_copy(buf[a].at[:, w], dst[a].at[:, w], sems.at[1, k])
+                  for k, (a, w) in enumerate(chunks)]
+        for copy in reads:
+            copy.start()
+        for read, write in zip(reads, writes):
+            read.wait()
+            write.start()
+        for copy in writes:
+            copy.wait()
+
+    return pl.pallas_call(
+        write,
+        out_shape=[jax.ShapeDtypeStruct(p.shape, F32) for p in parts],
+        in_specs=[hbm] * 4,
+        out_specs=[hbm] * 4,
+        scratch_shapes=[pltpu.VMEM(p.shape, F32) for p in parts] + [pltpu.SemaphoreType.DMA((2, len(chunks)))],
+        compiler_params=pltpu.CompilerParams(vmem_limit_bytes=60 * 1024 * 1024),
+    )(*parts)
 
 
 def solution(mesh):

time: 176 us -> 122 us (0.69)
  Pallas kernels: 167 us -> 119 us
  local copies, waits for them, and re-layouts: 7.57 us -> 0 us
    pallas_call x1, Pallas kernels: 167 us -> 117 us  [local(): pl.pallas_call(kernel, out_shape=(jax.ShapeDtypeStruct((64, 256), F32), j...]
    unnamed x4 -> x0, local copies, waits for them, and re-layouts: 7.57 us -> none
    pallas_call x0 -> x1, Pallas kernels: none -> 2.62 us  [local(): pl.pallas_call(write, out_shape=[jax.ShapeDtypeStruct(p.shape, F32) for p...]
where the time goes in v2:
time: 122 us; the launch traced here: 120 us
  Pallas kernels  119 us (98%)
    pallas_call x1, Pallas kernels, local(): pl.pallas_call(kernel, out_shape=(jax.ShapeDtypeStruct((64, 256), F32), j...  117 us
    pallas_call x1, Pallas kernels, local(): pl.pallas_call(write, out_shape=[jax.ShapeDtypeStruct(p.shape, F32) for p...  2.62 us

profile of v2, /device:TPU:1, one launch (start us, length us, event | category | flops | bytes accessed | tf_op | source)
XLA Modules:
  0.0 120.2 jit_solution(4170455145547534828)
XLA Ops:
  0.6 116.7 %shard_map.84 = (f32[64,256]{1,0:T(8,128)}, f32[64,256]{1,0:T(8,128)}, f32[64,512]{1,0:T(8,128)}, f32[64,8192]{1,0:T(8,128)}) custom-call(f32[64,2048]{1,0:T(8,128)} %g_hbm.1, f32[64,4096]{1,0:T(8,128)} %c_hbm.1, f32[64,8192]{1,0:T(8,128)} %r_hbm.1, s32[4,2048]{1,0:T(4,128)} %gm_hbm.1, s32[2,4096]{1,0:T(2,128)} %cm_hbm.1), custom_call_target="tpu_custom_call" | custom-call | tf_op jit(solution)/shard_map/pallas_call | solution.py:607
  117.4 2.6 %shard_map.85 = (f32[64,256]{1,0:T(8,128)}, f32[64,256]{1,0:T(8,128)}, f32[64,512]{1,0:T(8,128)}, f32[64,8192]{1,0:T(8,128)}) custom-call(f32[64,256]{1,0:T(8,128)} %get-tuple-element.8.refs_0_, f32[64,256]{1,0:T(8,128)} %get-tuple-element.9.refs_1_, f32[64,512]{1,0:T(8,128)} %get-tuple-element.10.refs_2_, f32[64,8192]{1,0:T(8,128)} %get-tuple-element.11.refs_3_), custom_call_target="tpu_custom_call" | custom-call | tf_op jit(solution)/shard_map/pallas_call | solution.py:672
